TPU v7x, 512 devices: a whole 4x8x8 slice. The times are simulated.
512 devices in a mesh: grp: 16 (over y, core), ops: 32 (over x, z).
Axes of the slice: x: 4, y: 8, z: 8, core: 2. Of those that a mesh axis runs over, the one named last changes fastest.
Arguments:
- op_embed: bfloat16 [131072, 256], P(('grp', 'ops')), may hold values from -6 to 6
- machine_embed: bfloat16 [8192, 256], P('grp'), may hold values from -6 to 6
- cotangent: bfloat16 [131072, 256], P(('grp', 'ops')), may hold values from -6 to 6
- w_query: bfloat16 [256, 256], replicated, may hold values from -0.375 to 0.375
- w_key: bfloat16 [256, 256], replicated, may hold values from -0.375 to 0.375
- w_value: bfloat16 [256, 256], replicated, may hold values from -0.375 to 0.375
- slot_local: int32 [512, 16], P(('grp', 'ops')), may hold values from 0 to 3
- counts: int32 [131072, 16], P(('grp', 'ops')), may hold values from 0 to 128, as said below
Outputs:
- op_grad: bfloat16 [131072, 256], P(('grp', 'ops'))
- machine_grad: float32 [8192, 256], P(('grp', 'ops'))
- grad_wq: float32 [256, 256], replicated
- grad_wk: float32 [256, 256], replicated
- grad_wv: float32 [256, 256], replicated
Inputs may be any that keep to these rules, and one draw needn't show every extreme that they name: The eligible machines of slot e's block for operation o are its first counts[o, e] machines; 0 means the operation has no eligible machine in that block.
All inputs are finite; a program needn't handle non-finite values.
Results may differ from a plain program's by a relative error of at most 0.0056.
Values may be sent and summed in bfloat16 or wider, within the bound.
No kernel may reach another device: no remote copies, remote signals or barrier semaphores. Data moves between devices by JAX's collectives and lax.ppermute only.
A program may use at most 64 MiB of HBM per device.

v0:
```python
import jax
import jax.numpy as jnp
from jax import lax
from jax.sharding import PartitionSpec as P

HEADS = 8
BLK = 128
mean_scale = 0.08838834764831845


def slot_grads(queries, cotangent4, key_rows, value_rows, lengths):
    head_size = queries.shape[2]
    inv_root = head_size ** (-0.5)
    scores = (
        jnp.einsum("ohc,mhc->ohm", queries, key_rows, preferred_element_type=jnp.float32) * inv_root
    )
    sigmoid_score = jax.nn.sigmoid(scores)
    columns = lax.broadcasted_iota(jnp.int32, scores.shape, 2)
    eligible = columns < lengths[:, None, None]
    gates = jnp.where(eligible, sigmoid_score, 0.0).astype(jnp.bfloat16)
    value_dot = jnp.einsum(
        "ohc,mhc->ohm", cotangent4, value_rows, preferred_element_type=jnp.float32
    )
    dscore = jnp.where(
        eligible, mean_scale * value_dot * sigmoid_score * (1.0 - sigmoid_score) * inv_root, 0.0
    ).astype(jnp.bfloat16)
    query_part = jnp.einsum("ohm,mhc->ohc", dscore, key_rows, preferred_element_type=jnp.float32)
    key_grad = jnp.einsum(
        "ohm,ohc->mhc", dscore, queries, preferred_element_type=jnp.float32
    ).astype(jnp.bfloat16)
    value_grad = (
        mean_scale
        * jnp.einsum("ohm,ohc->mhc", gates, cotangent4, preferred_element_type=jnp.float32)
    ).astype(jnp.bfloat16)
    return (query_part, key_grad, value_grad)


def per_device(op_embed, machine_embed, cotangent, w_query, w_key, w_value, slot_local, counts):
    groups = lax.axis_size("grp")
    ops_count = op_embed.shape[0]
    model_width = op_embed.shape[1]
    head_size = model_width // HEADS
    machine_rows = machine_embed.shape[0]
    blocks_here = machine_rows // BLK
    highest = lax.Precision.HIGHEST
    both_weights = jnp.concatenate([w_key, w_value], axis=1)
    queries = jnp.dot(op_embed, w_query, preferred_element_type=jnp.float32).astype(jnp.bfloat16)
    wanted = lax.all_to_all(
        slot_local.reshape(groups, 1), "grp", split_axis=0, concat_axis=0, tiled=True
    )
    wanted_ids = wanted[:, 0]
    picker = wanted_ids[:, None] == jnp.arange(blocks_here, dtype=jnp.int32)[None, :]
    local_pairs = jnp.dot(machine_embed, both_weights, preferred_element_type=jnp.float32).astype(
        jnp.bfloat16
    )
    outgoing = local_pairs.reshape(blocks_here, BLK, 2 * model_width)[wanted_ids]
    fetched = lax.all_to_all(outgoing, "grp", split_axis=0, concat_axis=0, tiled=True)
    key_slots = fetched[:, :, :model_width].reshape(groups, BLK, HEADS, head_size)
    value_slots = fetched[:, :, model_width:].reshape(groups, BLK, HEADS, head_size)
    query_heads = queries.reshape(ops_count, HEADS, head_size)
    cot_heads = cotangent.reshape(ops_count, HEADS, head_size)

    def per_slot(summed_q, pieces):
        key_rows, value_rows, lengths = pieces
        query_part, key_grad, value_grad = slot_grads(
            query_heads, cot_heads, key_rows, value_rows, lengths
        )
        return (
            summed_q + query_part,
            (key_grad.reshape(BLK, model_width), value_grad.reshape(BLK, model_width)),
        )

    start_q = jnp.zeros((ops_count, HEADS, head_size), jnp.float32)
    summed_q, (key_grads, value_grads) = lax.scan(
        per_slot, start_q, (key_slots, value_slots, counts.T)
    )
    grad_query = summed_q.astype(jnp.bfloat16).reshape(ops_count, model_width)
    op_grad = (
        cotangent.astype(jnp.float32)
        + jnp.dot(grad_query, w_query.T, preferred_element_type=jnp.float32)
    ).astype(jnp.bfloat16)
    wq_term = jnp.einsum("od,oe->de", op_embed, grad_query, preferred_element_type=jnp.float32)
    returned = lax.all_to_all(
        jnp.concatenate([key_grads, value_grads], axis=2),
        "grp",
        split_axis=0,
        concat_axis=0,
        tiled=True,
    )
    summed = jnp.einsum(
        "gb,gr->br",
        picker.astype(jnp.bfloat16),
        returned.reshape(groups, BLK * 2 * model_width),
        preferred_element_type=jnp.float32,
    )
    summed = summed.reshape(machine_rows, 2 * model_width)
    key_total = summed[:, :model_width]
    value_total = summed[:, model_width:]
    machine_part = jnp.dot(key_total, w_key.astype(jnp.float32).T, precision=highest) + jnp.dot(
        value_total, w_value.astype(jnp.float32).T, precision=highest
    )
    embed_f = machine_embed.astype(jnp.float32)
    wk_term = jnp.dot(embed_f.T, key_total, precision=highest)
    wv_term = jnp.dot(embed_f.T, value_total, precision=highest)
    summed_total = lax.psum(machine_part, "ops")
    share_rows = machine_rows // lax.axis_size("ops")
    first_row = lax.axis_index("ops") * share_rows
    machine_grad = lax.dynamic_slice_in_dim(summed_total, first_row, share_rows, 0)
    weight_sums = lax.psum((wq_term, wk_term, wv_term), ("grp", "ops"))
    shard_count = float(groups * lax.axis_size("ops"))
    grad_wq = weight_sums[0] / shard_count
    grad_wk = weight_sums[1] / shard_count
    grad_wv = weight_sums[2] / shard_count
    return (op_grad, machine_grad, grad_wq, grad_wk, grad_wv)


def solution(mesh):
    return jax.shard_map(
        per_device,
        mesh=mesh,
        in_specs=(
            P(("grp", "ops"), None),
            P("grp", None),
            P(("grp", "ops"), None),
            P(),
            P(),
            P(),
            P(("grp", "ops"), None),
            P(("grp", "ops"), None),
        ),
        out_specs=(P(("grp", "ops"), None), P(("grp", "ops"), None), P(), P(), P()),
        check_vma=False,
    )
```

profile of v0, /device:TPU:8, one launch (start us, length us, event | category | flops | bytes accessed | tf_op | source)
XLA Modules:
  0.0 657.2 jit_solution(9235457132968034616)
XLA Ops:
  7.2 1.4 copy.46
  8.6 9.1 %all-to-all-start = ((s32[16,1,1]{2,1,0:T(1,128)}), s32[16,1,1]{2,1,0:T(1,128)S(1)}, u32[]{:S(2)}, u32[]{:S(2)}) async-start(s32[16,1,1]{2,1,0:T(1,128)} %copy.46), calls=%async_computation | async-start | bytes 16384 | tf_op jit(solution)/shard_map/all_to_all | solution.py:48
  17.6 1.3 convolution_convert_fusion.1
  18.9 4.9 all-to-all-done
  24.2 2.0 gather_fusion
  26.2 5.1 all-to-all-start.1
  31.7 46.8 %all-to-all-done.1 = bf16[16,128,512]{2,1,0:T(8,128)(2,1)S(1)} async-done(((bf16[16,128,512]{2,1,0:T(8,128)(2,1)}), bf16[16,128,512]{2,1,0:T(8,128)(2,1)S(1)}, u32[]{:S(2)}, u32[]{:S(2)}) %all-to-all-start.1) | async-done | bytes 2097184 | tf_op jit(solution)/shard_map/all_to_all | solution.py:57
  78.6 1.6 fusion.38
  80.2 1.7 copy.47
  81.9 1.3 copy.48
  83.2 63.6 %while.15 = (s32[]{:T(128)}, f32[256,8,32]{0,2,1:T(8,128)S(1)}, bf16[16,128,256]{1,2,0:T(8,128)(2,1)}, bf16[16,128,256]{1,2,0:T(8,128)(2,1)}, bf16[16,128,8,32]{...) while((s32[]{:T(128)}, f32[256,8,32]{0,2,1:T(8,128)S(1)}, ...), condition=%wide.region_1.2_spmd.clone, body=%wide.region_0.1_spmd.clone.sunk | while | flops 87785472 | bytes 6361235 | solution.py:74
  84.4 1.3 fusion.80
  87.7 0.7 constant_dynamic-slice_fusion.3
  88.4 1.3 fusion.80
  91.7 0.7 constant_dynamic-slice_fusion.3
  92.4 1.3 fusion.80
  95.6 0.7 constant_dynamic-slice_fusion.3
  96.3 1.3 fusion.80
  100.3 1.3 fusion.80
  104.3 1.3 fusion.80
  108.2 1.3 fusion.80
  112.2 1.3 fusion.80
  116.2 1.3 fusion.80
  120.2 1.3 fusion.80
  124.1 1.3 fusion.80
  128.1 1.3 fusion.80
  132.1 1.3 fusion.80
  136.1 1.3 fusion.80
  140.1 1.3 fusion.80
  144.0 1.3 fusion.80
  146.8 3.1 pad_maximum_fusion
  149.9 6.9 %all-to-all-start.2 = ((bf16[16,128,512]{1,2,0:T(8,128)(2,1)}), bf16[16,128,512]{1,2,0:T(8,128)(2,1)}, u32[]{:S(2)}, u32[]{:S(2)}) async-start(bf16[16,128,512]{1,2,0:T(8,128)(2,1)} %pad_maximum_fusion), calls=%async_computation.2 | async-start | bytes 4194304 | tf_op jit(solution)/shard_map/all_to_all | solution.py:83
  156.8 0.9 convolution_bitcast_fusion.3
  157.7 46.3 %all-to-all-done.2 = bf16[16,128,512]{1,2,0:T(8,128)(2,1)} async-done(((bf16[16,128,512]{1,2,0:T(8,128)(2,1)}), bf16[16,128,512]{1,2,0:T(8,128)(2,1)}, u32[]{:S(2)}, u32[]{:S(2)}) %all-to-all-start.2) | async-done | bytes 2097184 | tf_op jit(solution)/shard_map/all_to_all | solution.py:83
  204.0 3.4 copy.57
  208.0 0.7 reshape.79
  208.7 1.3 convolution_bitcast_fusion.2
  210.0 1.3 convolution_bitcast_fusion.1
  211.9 1.2 convolution_add_fusion
  213.1 0.9 fusion.25
  214.0 274.6 %all-reduce.6.cloned.1.call-done = (f32[256,256]{0,1:T(8,128)}, f32[256,256]{0,1:T(8,128)}, f32[256,256]{0,1:T(8,128)}) async-done(((f32[256,256]{0,1:T(8,128)}, f32[256,256]{0,1:T(8,128)}, f32[256,256]{0,1:T(8,128)}), (f32[256,256]{0,1:T(8,128)}, f32[256,256]{0,1:T(8,128)}, f32[256,256]{0,1:T(8,128)})) %all-reduce.6.cloned.1.call-update) | async-done | bytes 786448 | tf_op jit(solution)/shard_map/psum | solution.py:109
  488.6 1.0 broadcast_multiply_fusion.2
  489.6 0.8 copy.51
  490.4 1.1 broadcast_multiply_fusion
  491.5 0.8 copy.52
  492.3 0.8 copy.53
  493.2 155.8 %all-reduce.4.cloned.1.call-done = f32[512,256]{1,0:T(8,128)} async-done(((f32[512,256]{1,0:T(8,128)}), f32[512,256]{1,0:T(8,128)}) %all-reduce.4.cloned.1.call-update) | async-done | bytes 524304 | tf_op jit(solution)/shard_map/psum | solution.py:105
  649.0 1.3 constant_dynamic-slice_fusion.1
  (128 shorter events, 42.0 us)
Async XLA Ops:
  7.2 10.5 %copy-start = (bf16[512,256]{1,0:T(8,128)(2,1)S(1)}, bf16[512,256]{1,0:T(8,128)(2,1)}, u32[]{:S(2)}) copy-start(bf16[512,256]{1,0:T(8,128)(2,1)} %param.11) | copy-start | bytes 786436
  8.6 15.3 %all-to-all-start = ((s32[16,1,1]{2,1,0:T(1,128)}), s32[16,1,1]{2,1,0:T(1,128)S(1)}, u32[]{:S(2)}, u32[]{:S(2)}) async-start(s32[16,1,1]{2,1,0:T(1,128)} %copy.46), calls=%async_computation | async-start | bytes 16384 | tf_op jit(solution)/shard_map/all_to_all | solution.py:48
  26.2 5.1 copy-start.6
  26.2 5.3 copy-start.2
  26.2 5.3 copy-start.4
  26.2 52.3 %all-to-all-start.1 = ((bf16[16,128,512]{2,1,0:T(8,128)(2,1)}), bf16[16,128,512]{2,1,0:T(8,128)(2,1)S(1)}, u32[]{:S(2)}, u32[]{:S(2)}) async-start(bf16[16,128,512]{2,1,0:T(8,128)(2,1)} %gather_fusion), calls=%async_computation.1 | async-start | bytes 4194304 | tf_op jit(solution)/shard_map/all_to_all | solution.py:57
  80.2 1.7 copy-start.1
  149.9 6.9 %copy-start.3 = (bf16[256,256]{1,0:T(8,128)(2,1)S(1)}, bf16[256,256]{1,0:T(8,128)(2,1)}, u32[]{:S(2)}) copy-start(bf16[256,256]{1,0:T(8,128)(2,1)} %param.10) | copy-start | bytes 393220
  149.9 54.2 %all-to-all-start.2 = ((bf16[16,128,512]{1,2,0:T(8,128)(2,1)}), bf16[16,128,512]{1,2,0:T(8,128)(2,1)}, u32[]{:S(2)}, u32[]{:S(2)}) async-start(bf16[16,128,512]{1,2,0:T(8,128)(2,1)} %pad_maximum_fusion), calls=%async_computation.2 | async-start | bytes 4194304 | tf_op jit(solution)/shard_map/all_to_all | solution.py:83
  156.8 331.9 %all-reduce.6.cloned.1.call-start = ((), (), s32[]{:S(2)}) async-start(), calls=%async_computation.4 | async-start | bytes 1572864 | tf_op jit(solution)/shard_map/psum | solution.py:109
  208.0 3.4 copy-start.8
  208.7 3.1 copy-start.9
  211.3 1.8 copy-start.5
  211.3 1.8 copy-start.7
  211.4 437.6 %all-reduce.4.cloned.1.call-start = ((), (), s32[]{:S(2)}) async-start(), calls=%async_computation.3 | async-start | bytes 1048576 | tf_op jit(solution)/shard_map/psum | solution.py:105
Sparse Core Ops, SparseCore 0:
  211.5 277.0 all-reduce.5
  492.0 156.9 all-reduce.3
where the time goes:
time: 659 us; the launch traced here: 657 us
  waiting for transfers between devices  529 us (80%)
  matrix products  48.8 us (7%)
  local copies, waits for them, and re-layouts  38.4 us (6%)
  starting transfers between devices  21.1 us (3%)
  between operations  14.3 us (2%)
    psum x1, waiting for transfers between devices, per_device(): weight_sums = lax.psum((wq_term, wk_term, wv_term), ('grp', 'ops'))  275 us
    psum x1, waiting for transfers between devices, per_device(): summed_total = lax.psum(machine_part, 'ops')  156 us
    all_to_all x1, waiting for transfers between devices, per_device(): lax.all_to_all(outgoing, 'grp', split_axis=0, concat_axis=0, tiled=True)  46.8 us
    all_to_all x1, waiting for transfers between devices, per_device(): lax.all_to_all(jnp.concatenate([key_grads, value_grads], axis=2), 'grp',...  46.3 us
    dot_general x16, matrix products, slot_grads(): jnp.einsum('ohc,mhc->ohm', cotangent4, value_rows, preferred_element_type...  20.9 us
  transfers between devices with their start and end apart: 5, of which 5 were waited for; matrix products, arithmetic and copies ran while one was open for 1% of the time, Pallas kernels for 0%

commit v1 on v0

--- a/solution.py
+++ b/solution.py
@@ -6,6 +6,15 @@
 HEADS = 8
 BLK = 128
 mean_scale = 0.08838834764831845
+
+
+def doubling_sum(x, name):
+    n_dev = lax.axis_size(name)
+    result, stride = (x, 1)
+    while stride < n_dev:
+        result = result + lax.ppermute(result, name, [(i, i ^ stride) for i in range(n_dev)])
+        stride = 2 * stride
+    return result
 
 
 def slot_grads(queries, cotangent4, key_rows, value_rows, lengths):
@@ -102,7 +111,7 @@
     embed_f = machine_embed.astype(jnp.float32)
     wk_term = jnp.dot(embed_f.T, key_total, precision=highest)
     wv_term = jnp.dot(embed_f.T, value_total, precision=highest)
-    summed_total = lax.psum(machine_part, "ops")
+    summed_total = doubling_sum(machine_part, "ops")
     share_rows = machine_rows // lax.axis_size("ops")
     first_row = lax.axis_index("ops") * share_rows
     machine_grad = lax.dynamic_slice_in_dim(summed_total, first_row, share_rows, 0)

time: 659 us -> 596 us (0.904)
  the two profiles are of different devices: /device:TPU:8 before, /device:TPU:17 now
where the time goes in v1:
time: 596 us; the launch traced here: 593 us
  waiting for transfers between devices  379 us (64%)
  matrix products  62.6 us (11%)
  blocking collectives  54.9 us (9%)
  starting transfers between devices  40 us (7%)
  local copies, waits for them, and re-layouts  37.4 us (6%)
  between operations  14.3 us (2%)
    psum x1, waiting for transfers between devices, per_device(): weight_sums = lax.psum((wq_term, wk_term, wv_term), ('grp', 'ops'))  264 us
    ppermute x5, waiting for transfers between devices, doubling_sum(): lax.ppermute(result, name, [(i, i ^ stride) for i in range(n_dev)])  64.1 us
    all_to_all x1, blocking collectives, per_device(): lax.all_to_all(jnp.concatenate([key_grads, value_grads], axis=2), 'grp',...  54.9 us
    all_to_all x1, waiting for transfers between devices, per_device(): lax.all_to_all(outgoing, 'grp', split_axis=0, concat_axis=0, tiled=True)  47.1 us
    ppermute x5, starting transfers between devices, doubling_sum(): lax.ppermute(result, name, [(i, i ^ stride) for i in range(n_dev)])  23.7 us
    dot_general x16, matrix products, slot_grads(): jnp.einsum('ohc,mhc->ohm', queries, key_rows, preferred_element_type=jnp....  21.3 us
    dot_general x16, matrix products, slot_grads(): jnp.einsum('ohm,mhc->ohc', dscore, key_rows, preferred_element_type=jnp.f...  17 us
  transfers between devices with their start and end apart: 8, of which 7 were waited for; matrix products, arithmetic and copies ran while one was open for 2% of the time, Pallas kernels for 0%

profile of v1, /device:TPU:17, one launch (start us, length us, event | category | flops | bytes accessed | tf_op | source)
XLA Modules:
  0.0 593.3 jit_solution(13893918019098432157)
XLA Ops:
  7.2 1.4 copy.46
  8.6 9.2 %all-to-all-start = ((s32[16,1,1]{2,1,0:T(1,128)}), s32[16,1,1]{2,1,0:T(1,128)S(1)}, u32[]{:S(2)}, u32[]{:S(2)}) async-start(s32[16,1,1]{2,1,0:T(1,128)} %copy.46), calls=%async_computation | async-start | bytes 16384 | tf_op jit(solution)/shard_map/all_to_all | solution.py:57
  17.8 1.3 convolution_convert_fusion.1
  19.1 3.8 all-to-all-done
  23.2 2.0 gather_fusion
  25.2 6.9 %all-to-all-start.1 = ((bf16[16,128,512]{2,1,0:T(8,128)(2,1)}), bf16[16,128,512]{2,1,0:T(8,128)(2,1)}, u32[]{:S(2)}, u32[]{:S(2)}) async-start(bf16[16,128,512]{2,1,0:T(8,128)(2,1)} %gather_fusion), calls=%async_computation.1 | async-start | bytes 4194304 | tf_op jit(solution)/shard_map/all_to_all | solution.py:66
  32.6 47.1 %all-to-all-done.1 = bf16[16,128,512]{2,1,0:T(8,128)(2,1)} async-done(((bf16[16,128,512]{2,1,0:T(8,128)(2,1)}), bf16[16,128,512]{2,1,0:T(8,128)(2,1)}, u32[]{:S(2)}, u32[]{:S(2)}) %all-to-all-start.1) | async-done | bytes 2097184 | tf_op jit(solution)/shard_map/all_to_all | solution.py:66
  79.8 1.7 fusion.38
  81.4 1.3 copy.47
  83.4 77.3 %while.15 = (s32[]{:T(128)}, f32[256,8,32]{0,2,1:T(8,128)S(1)}, bf16[16,128,256]{1,2,0:T(8,128)(2,1)}, bf16[16,128,256]{1,2,0:T(8,128)(2,1)}, bf16[16,128,8,32]{...) while((s32[]{:T(128)}, f32[256,8,32]{0,2,1:T(8,128)S(1)}, ...), condition=%wide.region_1.2_spmd.clone, body=%wide.region_0.1_spmd.clone.sunk | while | flops 87785472 | bytes 6361235 | solution.py:83
  83.4 1.3 fusion.79
  88.3 1.3 fusion.79
  93.1 1.3 fusion.79
  95.6 1.1 fusion.81
  97.9 1.3 fusion.79
  100.5 1.1 fusion.81
  102.8 1.3 fusion.79
  107.6 1.3 fusion.79
  112.4 1.3 fusion.79
  117.3 1.3 fusion.79
  122.1 1.3 fusion.79
  126.9 1.3 fusion.79
  131.8 1.3 fusion.79
  134.3 1.1 fusion.81
  136.6 1.3 fusion.79
  141.4 1.3 fusion.79
  143.9 1.1 fusion.81
  146.3 1.3 fusion.79
  151.1 1.3 fusion.79
  155.9 1.3 fusion.79
  160.7 1.7 pad_maximum_fusion
  162.5 54.9 %all_to_all.22 = bf16[16,128,512]{1,2,0:T(8,128)(2,1)} all-to-all(bf16[16,128,512]{1,2,0:T(8,128)(2,1)S(1)} %pad_maximum_fusion), channel_id=1, replica_groups=mesh['grp'=16,'ops'=32] {'grp'}, dimensions={0} | all-to-all | bytes 4194304 | tf_op jit(solution)/shard_map/all_to_all | solution.py:92
  217.4 3.4 copy.57
  220.8 1.6 fusion.34
  222.4 2.0 reshape.79
  225.2 2.4 collective-permute-start
  227.7 12.5 %collective-permute-done = f32[512,256]{1,0:T(8,128)S(1)} collective-permute-done((f32[512,256]{1,0:T(8,128)S(1)}, f32[512,256]{1,0:T(8,128)S(1)}, u32[]{:S(2)}, u32[]{:S(2)}) %collective-permute-start) | collective-permute-done | bytes 524320 | tf_op jit(solution)/shard_map/ppermute | solution.py:15
  240.3 5.2 collective-permute-start.1
  245.4 22.7 %collective-permute-done.1 = f32[512,256]{1,0:T(8,128)S(1)} collective-permute-done((f32[512,256]{1,0:T(8,128)S(1)}, f32[512,256]{1,0:T(8,128)S(1)}, u32[]{:S(2)}, u32[]{:S(2)}) %collective-permute-start.1) | collective-permute-done | bytes 524320 | tf_op jit(solution)/shard_map/ppermute | solution.py:15
  268.2 8.1 %collective-permute-start.2 = (f32[512,256]{1,0:T(8,128)S(1)}, f32[512,256]{1,0:T(8,128)S(1)}, u32[]{:S(2)}, u32[]{:S(2)}) collective-permute-start(f32[512,256]{1,0:T(8,128)S(1)} %add.56), channel_id=1, source_target_pairs={{0,4},{1,5},{2,6},{3,7},{4,0},{5,1},{6,2},{7,3},{8,12},{9,13},{10,... | collective-permute-start | bytes 1572872 | tf_op jit(solution)/shard_map/ppermute | solution.py:15
  277.3 21.3 %collective-permute-done.2 = f32[512,256]{1,0:T(8,128)S(1)} collective-permute-done((f32[512,256]{1,0:T(8,128)S(1)}, f32[512,256]{1,0:T(8,128)S(1)}, u32[]{:S(2)}, u32[]{:S(2)}) %collective-permute-start.2) | collective-permute-done | bytes 524320 | tf_op jit(solution)/shard_map/ppermute | solution.py:15
  298.7 3.3 collective-permute-start.3
  302.0 1.3 convolution_bitcast_fusion.2
  303.3 1.3 convolution_bitcast_fusion.1
  304.6 7.5 %collective-permute-done.3 = f32[512,256]{1,0:T(8,128)S(1)} collective-permute-done((f32[512,256]{1,0:T(8,128)S(1)}, f32[512,256]{1,0:T(8,128)S(1)}, u32[]{:S(2)}, u32[]{:S(2)}) %collective-permute-start.3) | collective-permute-done | bytes 524320 | tf_op jit(solution)/shard_map/ppermute | solution.py:15
  312.2 4.7 collective-permute-start.4
  317.8 263.5 %all-reduce.3.cloned.1.call-done = (f32[256,256]{0,1:T(8,128)}, f32[256,256]{0,1:T(8,128)}, f32[256,256]{0,1:T(8,128)}) async-done(((f32[256,256]{0,1:T(8,128)}, f32[256,256]{0,1:T(8,128)}, f32[256,256]{0,1:T(8,128)}), (f32[256,256]{0,1:T(8,128)}, f32[256,256]{0,1:T(8,128)}, f32[256,256]{0,1:T(8,128)})) %all-reduce.3.cloned.1.call-update) | async-done | bytes 786448 | tf_op jit(solution)/shard_map/psum | solution.py:118
  583.1 1.1 broadcast_multiply_fusion
  (134 shorter events, 59.8 us)
Async XLA Ops:
  7.2 10.6 %copy-start = (bf16[512,256]{1,0:T(8,128)(2,1)S(1)}, bf16[512,256]{1,0:T(8,128)(2,1)}, u32[]{:S(2)}) copy-start(bf16[512,256]{1,0:T(8,128)(2,1)} %param.11) | copy-start | bytes 786436
  8.6 14.3 %all-to-all-start = ((s32[16,1,1]{2,1,0:T(1,128)}), s32[16,1,1]{2,1,0:T(1,128)S(1)}, u32[]{:S(2)}, u32[]{:S(2)}) async-start(s32[16,1,1]{2,1,0:T(1,128)} %copy.46), calls=%async_computation | async-start | bytes 16384 | tf_op jit(solution)/shard_map/all_to_all | solution.py:57
  25.2 7.0 %copy-start.4 = (bf16[256,256]{1,0:T(8,128)(2,1)S(1)}, bf16[256,256]{1,0:T(8,128)(2,1)}, u32[]{:S(2)}) copy-start(bf16[256,256]{1,0:T(8,128)(2,1)} %param.12) | copy-start | bytes 393220
  25.2 7.1 %copy-start.1 = (bf16[256,256]{1,0:T(8,128)(2,1)S(1)}, bf16[256,256]{1,0:T(8,128)(2,1)}, u32[]{:S(2)}) copy-start(bf16[256,256]{1,0:T(8,128)(2,1)} %param.10) | copy-start | bytes 393220
  25.2 7.1 %copy-start.2 = (bf16[256,256]{1,0:T(8,128)(2,1)S(1)}, bf16[256,256]{1,0:T(8,128)(2,1)}, u32[]{:S(2)}) copy-start(bf16[256,256]{1,0:T(8,128)(2,1)} %param.13) | copy-start | bytes 393220
  25.2 54.5 %all-to-all-start.1 = ((bf16[16,128,512]{2,1,0:T(8,128)(2,1)}), bf16[16,128,512]{2,1,0:T(8,128)(2,1)}, u32[]{:S(2)}, u32[]{:S(2)}) async-start(bf16[16,128,512]{2,1,0:T(8,128)(2,1)} %gather_fusion), calls=%async_computation.1 | async-start | bytes 4194304 | tf_op jit(solution)/shard_map/all_to_all | solution.py:66
  32.2 549.1 %all-reduce.3.cloned.1.call-start = ((), (), s32[]{:S(2)}) async-start(), calls=%async_computation.3 | async-start | bytes 1572864 | tf_op jit(solution)/shard_map/psum | solution.py:118
  220.8 3.6 copy-start.6
  222.3 2.4 copy-start.7
  225.2 15.0 %collective-permute-start = (f32[512,256]{1,0:T(8,128)S(1)}, f32[512,256]{1,0:T(8,128)S(1)}, u32[]{:S(2)}, u32[]{:S(2)}) collective-permute-start(f32[512,256]{1,0:T(8,128)S(1)} %convolution_add_fusion), channel_id=1, source_target_pairs={{0,1},{1,0},{2,3},{3,2},{4,5},{5,4},{6,7},{7,6},{8,9},{9,8},{10,11... | collective-permute-start | bytes 1572872 | tf_op jit(solution)/shard_map/ppermute | solution.py:15
  240.3 27.9 %collective-permute-start.1 = (f32[512,256]{1,0:T(8,128)S(1)}, f32[512,256]{1,0:T(8,128)S(1)}, u32[]{:S(2)}, u32[]{:S(2)}) collective-permute-start(f32[512,256]{1,0:T(8,128)S(1)} %add.55), channel_id=1, source_target_pairs={{0,2},{1,3},{2,0},{3,1},{4,6},{5,7},{6,4},{7,5},{8,10},{9,11},{10,... | collective-permute-start | bytes 1572872 | tf_op jit(solution)/shard_map/ppermute | solution.py:15
  268.2 30.4 %collective-permute-start.2 = (f32[512,256]{1,0:T(8,128)S(1)}, f32[512,256]{1,0:T(8,128)S(1)}, u32[]{:S(2)}, u32[]{:S(2)}) collective-permute-start(f32[512,256]{1,0:T(8,128)S(1)} %add.56), channel_id=1, source_target_pairs={{0,4},{1,5},{2,6},{3,7},{4,0},{5,1},{6,2},{7,3},{8,12},{9,13},{10,... | collective-permute-start | bytes 1572872 | tf_op jit(solution)/shard_map/ppermute | solution.py:15
  298.7 18.2 %copy-start.3 = (bf16[256,256]{1,0:T(8,128)(2,1)S(1)}, bf16[256,256]{1,0:T(8,128)(2,1)}, u32[]{:S(2)}) copy-start(bf16[256,256]{1,0:T(8,128)(2,1)} %param.13) | copy-start | bytes 393220
  298.7 18.2 %copy-start.5 = (bf16[256,256]{1,0:T(8,128)(2,1)S(1)}, bf16[256,256]{1,0:T(8,128)(2,1)}, u32[]{:S(2)}) copy-start(bf16[256,256]{1,0:T(8,128)(2,1)} %param.12) | copy-start | bytes 393220
  298.7 13.5 %collective-permute-start.3 = (f32[512,256]{1,0:T(8,128)S(1)}, f32[512,256]{1,0:T(8,128)S(1)}, u32[]{:S(2)}, u32[]{:S(2)}) collective-permute-start(f32[512,256]{1,0:T(8,128)S(1)} %add.57), channel_id=1, source_target_pairs={{0,8},{1,9},{2,10},{3,11},{4,12},{5,13},{6,14},{7,15},{8,0},{9,1},... | collective-permute-start | bytes 1572872 | tf_op jit(solution)/shard_map/ppermute | solution.py:15
  312.2 273.7 %collective-permute-start.4 = (f32[512,256]{1,0:T(8,128)S(1)}, f32[512,256]{1,0:T(8,128)S(1)}, u32[]{:S(2)}, u32[]{:S(2)}) collective-permute-start(f32[512,256]{1,0:T(8,128)S(1)} %add.58), channel_id=1, source_target_pairs={{0,16},{1,17},{2,18},{3,19},{4,20},{5,21},{6,22},{7,23},{8,24},{9,... | collective-permute-start | bytes 1572872 | tf_op jit(solution)/shard_map/ppermute | solution.py:15
Sparse Core Ops, SparseCore 0:
  304.7 276.5 all-reduce.2
